TPU v7x, 32 devices: a whole 2x2x4 slice. The times are simulated.
32 devices in a mesh: dp: 16 (over z, y, x), seq: 2 (over core).
Axes of the slice: x: 2, y: 2, z: 4, core: 2. Of those that a mesh axis runs over, the one named last changes fastest.
Arguments:
- layer_input: bfloat16 [16, 256, 1088], P('dp', 'seq'), may hold values from -6 to 6
- segments: int32 [16, 256], P('dp'), may hold values from 0 to 3, never falling along the last dimension, each value on 1 to 128 neighbouring positions
- w_attn: bfloat16 [3551232], P(('dp', 'seq')), may hold values from -1 to 1
- w_out: bfloat16 [1183744], P(('dp', 'seq')), may hold values from -1.5 to 1.5
- w_fc: bfloat16 [4734976], P(('dp', 'seq')), may hold values from -0.1875 to 0.1875
- w_proj: bfloat16 [4734976], P(('dp', 'seq')), may hold values from -0.09375 to 0.09375
- norm_params: bfloat16 [4352], P(('dp', 'seq')), may hold values from -1 to 3
- lin_bias: bfloat16 [4352], P(('dp', 'seq')), may hold values from -3 to 3
- fc_bias: bfloat16 [4352], P(('dp', 'seq')), may hold values from -3 to 3
- out_cotangent: bfloat16 [16, 256, 1088], P('dp', 'seq'), may hold values from -6 to 6
Outputs:
- layer_output: bfloat16 [16, 256, 1088], P('dp', 'seq')
- input_grad: float32 [16, 256, 1088], P('dp', 'seq')
- w_attn_grad: float32 [3551232], P(('dp', 'seq'))
- w_out_grad: float32 [1183744], P(('dp', 'seq'))
- w_fc_grad: float32 [4734976], P(('dp', 'seq'))
- w_proj_grad: float32 [4734976], P(('dp', 'seq'))
- norm_grad: float32 [4352], P(('dp', 'seq'))
- bias_grad: float32 [4352], P(('dp', 'seq'))
- fc_bias_grad: float32 [4352], P(('dp', 'seq'))
Inputs may be any that keep to these rules, and one draw needn't show every extreme that they name: `segments`: along each sequence the numbers never fall; each number marks one document.
All inputs are finite; a program needn't handle non-finite values.
Results may differ from a plain program's by a relative error of at most 0.011.
Values may be sent and summed in bfloat16 or wider, within the bound.
A program may use at most 320 MiB of HBM per device.

v0:
```python
import jax
import jax.numpy as jnp
from jax import lax
from jax.sharding import PartitionSpec as P

HD = 64
FF = 4352


GELU_C = 0.7978845608028654
NORM_EPS = 1e-05


def gelu_parts(inputs):
    tanh_value = jnp.tanh(GELU_C * (inputs + 0.044715 * inputs * inputs * inputs))
    value = 0.5 * inputs * (1.0 + tanh_value)
    slope = 0.5 * (1.0 + tanh_value) + 0.5 * inputs * (1.0 - tanh_value * tanh_value) * GELU_C * (
        1.0 + 3.0 * 0.044715 * inputs * inputs
    )
    return (value, slope)


def layer_norm(inputs, gains, offsets):
    average = jnp.mean(inputs, axis=-1, keepdims=True)
    centred = inputs - average
    inv_std = lax.rsqrt(jnp.mean(centred * centred, axis=-1, keepdims=True) + NORM_EPS)
    x_hat = centred * inv_std
    return (x_hat * gains + offsets, x_hat, inv_std)


def norm_back(grad_out, x_hat, inv_std, gains):
    grad_hat = grad_out * gains
    grad_in = inv_std * (
        grad_hat
        - jnp.mean(grad_hat, axis=-1, keepdims=True)
        - x_hat * jnp.mean(grad_hat * x_hat, axis=-1, keepdims=True)
    )
    return (grad_in, jnp.sum(grad_out * x_hat, axis=0), jnp.sum(grad_out, axis=0))


def score_block(queries, key_rows, allowed):
    scores = jnp.einsum(
        "qhd,khd->hqk", queries, key_rows, preferred_element_type=jnp.float32
    ) * HD ** (-0.5)
    return jnp.where(allowed[None], scores, -1e30)


def outer_sum(left, right):
    return jnp.einsum("na,nb->ab", left, right, preferred_element_type=jnp.float32)


def flat_term(left, right):
    block = outer_sum(left, right).reshape(-1)
    return block


def shard_rows(left, right, count, shard):
    return flat_term(left, right).reshape(count, shard)


def vector_rows(vector, count, shard):
    return vector.reshape(count, shard)


def per_device(
    layer_input,
    segments,
    w_attn,
    w_out,
    w_fc,
    w_proj,
    norm_params,
    lin_bias,
    fc_bias,
    out_cotangent,
):
    tokens = layer_input.shape[1]
    width = layer_input.shape[2]
    heads = width // HD
    place = lax.axis_index("seq")
    first = place * tokens
    full = (
        lax.all_gather(w_attn, ("dp", "seq"), axis=0, tiled=True),
        lax.all_gather(w_out, ("dp", "seq"), axis=0, tiled=True),
        lax.all_gather(w_fc, ("dp", "seq"), axis=0, tiled=True),
        lax.all_gather(w_proj, ("dp", "seq"), axis=0, tiled=True),
        lax.all_gather(norm_params, ("dp", "seq"), axis=0, tiled=True),
        lax.all_gather(lin_bias, ("dp", "seq"), axis=0, tiled=True),
        lax.all_gather(fc_bias, ("dp", "seq"), axis=0, tiled=True),
    )
    w_qkv = full[0].reshape(width, 3 * width)
    w_o = full[1].reshape(width, width)
    w_up = full[2].reshape(width, FF)
    w_down = full[3].reshape(FF, width)
    norms = full[4].astype(jnp.float32).reshape(4, width)
    biases = full[5].astype(jnp.float32).reshape(4, width)
    up_bias = full[6].astype(jnp.float32)
    inputs_f = layer_input[0].astype(jnp.float32)
    normed1, x_hat1, inv_std1 = layer_norm(inputs_f, norms[0], norms[1])
    act_in1 = normed1.astype(jnp.bfloat16)
    projected = jnp.dot(act_in1, w_qkv, preferred_element_type=jnp.float32)
    queries = (projected[:, :width] + biases[0]).astype(jnp.bfloat16)
    own_keys = projected[:, width : 2 * width].astype(jnp.bfloat16)
    own_values = (projected[:, 2 * width :] + biases[1]).astype(jnp.bfloat16)
    key_rows, value_rows = (
        lax.all_gather(own_keys, "seq", axis=0, tiled=True),
        lax.all_gather(own_values, "seq", axis=0, tiled=True),
    )
    key_count = key_rows.shape[0]
    key_pos = jnp.arange(key_count)
    query_pos = first + jnp.arange(tokens)
    padded_seg = jnp.concatenate([jnp.full((tokens,), -1, jnp.int32), segments[0]])
    key_seg = lax.dynamic_slice_in_dim(padded_seg, tokens, key_count)
    query_seg = lax.dynamic_slice_in_dim(segments[0], first, tokens)
    allowed = (key_pos[None, :] <= query_pos[:, None]) & (key_seg[None, :] == query_seg[:, None])
    q_heads = queries.reshape(tokens, heads, HD)
    k_heads = key_rows.reshape(key_count, heads, HD)
    v_heads = value_rows.reshape(key_count, heads, HD)
    scores = score_block(q_heads, k_heads, allowed)
    top_score = jnp.max(scores, axis=-1, keepdims=True)
    log_total = top_score + jnp.log(jnp.sum(jnp.exp(scores - top_score), axis=-1, keepdims=True))
    attn_probs = jnp.exp(scores - log_total).astype(jnp.bfloat16)
    attended = jnp.einsum("hqk,khd->qhd", attn_probs, v_heads, preferred_element_type=jnp.float32)
    attended = attended.reshape(tokens, width).astype(jnp.bfloat16)
    resid = inputs_f + jnp.dot(attended, w_o, preferred_element_type=jnp.float32) + biases[2]
    normed2, x_hat2, inv_std2 = layer_norm(resid, norms[2], norms[3])
    act_in2 = normed2.astype(jnp.bfloat16)
    hidden_pre = jnp.dot(act_in2, w_up, preferred_element_type=jnp.float32) + up_bias
    hidden_act, hidden_slope = gelu_parts(hidden_pre)
    hidden_b = hidden_act.astype(jnp.bfloat16)
    result = (
        resid + jnp.dot(hidden_b, w_down, preferred_element_type=jnp.float32) + biases[3]
    ).astype(jnp.bfloat16)
    back = (
        lax.all_gather(w_fc, ("dp", "seq"), axis=0, tiled=True),
        lax.all_gather(w_proj, ("dp", "seq"), axis=0, tiled=True),
        lax.all_gather(w_attn, ("dp", "seq"), axis=0, tiled=True),
        lax.all_gather(w_out, ("dp", "seq"), axis=0, tiled=True),
        lax.all_gather(norm_params, ("dp", "seq"), axis=0, tiled=True),
    )
    w_up_b = back[0].reshape(width, FF)
    w_down_b = back[1].reshape(FF, width)
    w_qkv_b = back[2].reshape(width, 3 * width)
    w_o_b = back[3].reshape(width, width)
    norms_b = back[4].astype(jnp.float32).reshape(4, width)
    cotangent = out_cotangent[0]
    grad_out = cotangent.astype(jnp.float32)
    grad_bp = jnp.sum(grad_out, axis=0)
    grad_hidden = (
        jnp.einsum("nd,fd->nf", cotangent, w_down_b, preferred_element_type=jnp.float32)
        * hidden_slope
    )
    grad_hidden_b = grad_hidden.astype(jnp.bfloat16)
    grad_up_bias = jnp.sum(grad_hidden, axis=0)
    proj_shard = w_proj.shape[0]
    fc_shard = w_fc.shape[0]
    fcb_shard = fc_bias.shape[0]
    mlp_sums = lax.psum_scatter(
        jnp.concatenate(
            [
                shard_rows(hidden_b, cotangent, lax.axis_size(("dp", "seq")) * 1, proj_shard),
                shard_rows(act_in2, grad_hidden_b, lax.axis_size(("dp", "seq")) * 1, fc_shard),
                vector_rows(grad_up_bias, lax.axis_size(("dp", "seq")) * 1, fcb_shard),
            ],
            axis=1,
        ),
        ("dp", "seq"),
        scatter_dimension=0,
        tiled=True,
    )[0]
    grad_norm2 = jnp.einsum("nf,df->nd", grad_hidden_b, w_up_b, preferred_element_type=jnp.float32)
    grad_resid_n, grad_g2, grad_b2 = norm_back(grad_norm2, x_hat2, inv_std2, norms_b[2])
    grad_resid = grad_out + grad_resid_n
    grad_resid_b = grad_resid.astype(jnp.bfloat16)
    grad_bo = jnp.sum(grad_resid, axis=0)
    grad_att = jnp.einsum(
        "ne,de->nd", grad_resid_b, w_o_b, preferred_element_type=jnp.float32
    ).astype(jnp.bfloat16)
    grad_att_heads = grad_att.reshape(tokens, heads, HD)
    probs_full = jnp.exp(score_block(q_heads, k_heads, allowed) - log_total)
    probs_b = probs_full.astype(jnp.bfloat16)
    grad_probs = jnp.einsum(
        "qhd,khd->hqk", grad_att_heads, v_heads, preferred_element_type=jnp.float32
    )
    delta = jnp.sum(probs_full * grad_probs, axis=-1, keepdims=True)
    grad_scores = (probs_full * (grad_probs - delta) * HD ** (-0.5)).astype(jnp.bfloat16)
    grad_q = jnp.einsum(
        "hqk,khd->qhd", grad_scores, k_heads, preferred_element_type=jnp.float32
    ).reshape(tokens, width)
    grad_k_all = jnp.einsum(
        "hqk,qhd->khd", grad_scores, q_heads, preferred_element_type=jnp.float32
    ).reshape(key_count, width)
    grad_v_all = jnp.einsum(
        "hqk,qhd->khd", probs_b, grad_att_heads, preferred_element_type=jnp.float32
    ).reshape(key_count, width)
    grad_k, grad_v = (
        lax.psum_scatter(
            grad_k_all.astype(jnp.bfloat16), "seq", scatter_dimension=0, tiled=True
        ).astype(jnp.float32),
        lax.psum_scatter(
            grad_v_all.astype(jnp.bfloat16), "seq", scatter_dimension=0, tiled=True
        ).astype(jnp.float32),
    )
    grad_proj_b = jnp.concatenate([grad_q, grad_k, grad_v], axis=1).astype(jnp.bfloat16)
    grad_norm1 = jnp.einsum("ne,de->nd", grad_proj_b, w_qkv_b, preferred_element_type=jnp.float32)
    grad_in_n, grad_g1, grad_b1 = norm_back(grad_norm1, x_hat1, inv_std1, norms_b[0])
    grad_input = grad_resid + grad_in_n
    norm_terms = jnp.concatenate([grad_g1, grad_b1, grad_g2, grad_b2])
    bias_terms = jnp.concatenate(
        [jnp.sum(grad_q, axis=0), jnp.sum(grad_v, axis=0), grad_bo, grad_bp]
    )
    qkv_shard = w_attn.shape[0]
    out_shard = w_out.shape[0]
    small_shard = norm_params.shape[0]
    count = lax.axis_size(("dp", "seq")) * 1
    attn_sums = lax.psum_scatter(
        jnp.concatenate(
            [
                shard_rows(act_in1, grad_proj_b, count, qkv_shard),
                shard_rows(attended, grad_resid_b, count, out_shard),
                vector_rows(norm_terms, count, small_shard),
                vector_rows(bias_terms, count, small_shard),
            ],
            axis=1,
        ),
        ("dp", "seq"),
        scatter_dimension=0,
        tiled=True,
    )[0]
    qkv_sums = attn_sums[:qkv_shard]
    out_sums = attn_sums[qkv_shard : qkv_shard + out_shard]
    norm_sums = attn_sums[qkv_shard + out_shard : qkv_shard + out_shard + small_shard]
    bias_sums = attn_sums[qkv_shard + out_shard + small_shard :]
    proj_sums = mlp_sums[:proj_shard]
    fc_sums = mlp_sums[proj_shard : proj_shard + fc_shard]
    fcb_sums = mlp_sums[proj_shard + fc_shard :]
    return (
        result[None],
        grad_input[None],
        qkv_sums,
        out_sums,
        fc_sums,
        proj_sums,
        norm_sums,
        bias_sums,
        fcb_sums,
    )


def solution(mesh):
    return jax.shard_map(
        per_device,
        mesh=mesh,
        in_specs=(
            P("dp", "seq", None),
            P("dp", None),
            P(("dp", "seq")),
            P(("dp", "seq")),
            P(("dp", "seq")),
            P(("dp", "seq")),
            P(("dp", "seq")),
            P(("dp", "seq")),
            P(("dp", "seq")),
            P("dp", "seq", None),
        ),
        out_specs=(
            P("dp", "seq", None),
            P("dp", "seq", None),
            P(("dp", "seq")),
            P(("dp", "seq")),
            P(("dp", "seq")),
            P(("dp", "seq")),
            P(("dp", "seq")),
            P(("dp", "seq")),
            P(("dp", "seq")),
        ),
        check_vma=False,
    )
```

profile of v0, /device:TPU:0, one launch (start us, length us, event | category | flops | bytes accessed | tf_op | source)
XLA Modules:
  0.0 1725.8 jit_solution(16161380731343247772)
XLA Ops:
  20.5 43.5 %all-reduce.6 = (bf16[4352]{0:T(1024)(128)(2,1)S(1)}, bf16[4352]{0:T(1024)(128)(2,1)S(1)}, bf16[4352]{0:T(1024)(128)(2,1)S(1)}) all-reduce(bf16[4352]{0:T(1024)(128)(2,1)S(1)} %dynamic-update-slice, bf16[4352]{0:T(1024)(128)(2,1)S(1)} %dynamic-update-slice.1, ...), channel_id=1, replica_groups=mesh['dp'=16,'seq'=2] {'dp','seq'}, use_global_device_ids=true, to_apply=%add | all-reduce | flops 13056 | bytes 52224
  65.3 13.0 all-gather.11.cloned.1.call-done
  78.3 50.9 %reduce.3 = bf16[32,36992]{1,0:T(8,128)(2,1)} reduce(bf16[32,1,36992]{2,1,0:T(2,128)(2,1)} %all-gather.11.cloned.1.call-done, bf16[]{:T(256)} %constant.65), dimensions={1}, to_apply=%all-gather.1.reduce_sub_computation | reduce | bytes 4734978 | tf_op jit(solution)/shard_map/all_gather | solution.py:84
  133.2 49.9 %all-gather.9.cloned.1.call-done = bf16[32,1,110976]{2,1,0:T(2,128)(2,1)} async-done(((bf16[1,1,110976]{2,1,0:T(2,128)(2,1)}), bf16[32,1,110976]{2,1,0:T(2,128)(2,1)}) %all-gather.9.cloned.1.call-update) | async-done | bytes 7102480 | tf_op jit(solution)/shard_map/all_gather | solution.py:83
  183.1 130.0 %reduce.2 = bf16[32,110976]{1,0:T(8,128)(2,1)} reduce(bf16[32,1,110976]{2,1,0:T(2,128)(2,1)} %all-gather.9.cloned.1.call-done, bf16[]{:T(256)} %constant.65), dimensions={1}, to_apply=%all-gather.reduce_sub_computation | reduce | bytes 14204930 | tf_op jit(solution)/shard_map/all_gather | solution.py:83
  313.1 9.6 reshape.233
  338.4 156.2 %reduce.5 = bf16[32,147968]{1,0:T(8,128)(2,1)} reduce(bf16[32,1,147968]{2,1,0:T(2,128)(2,1)} %all-gather.15.cloned.1.call-done, bf16[]{:T(256)} %constant.65), dimensions={1}, to_apply=%all-gather.3.reduce_sub_computation | reduce | bytes 18939906 | tf_op jit(solution)/shard_map/all_gather | solution.py:86
  494.6 11.8 reshape.239
  506.4 156.5 %reduce.4 = bf16[32,147968]{1,0:T(8,128)(2,1)} reduce(bf16[32,1,147968]{2,1,0:T(2,128)(2,1)} %all-gather.13.cloned.1.call-done, bf16[]{:T(256)} %constant.65), dimensions={1}, to_apply=%all-gather.2.reduce_sub_computation | reduce | bytes 18939906 | tf_op jit(solution)/shard_map/all_gather | solution.py:85
  662.9 17.3 %reshape.238 = bf16[1088,4352]{1,0:T(8,128)(2,1)} reshape(bf16[32,147968]{1,0:T(8,128)(2,1)} %reduce.4) | data formatting | bytes 18939904 | tf_op jit(solution)/shard_map/reshape | solution.py:93
  685.8 7.7 fusion.102
  696.3 8.3 fusion.51
  710.5 16.2 fusion.20
  729.0 24.2 %reshape_reshape.15 = f32[32,147968]{1,0:T(8,128)} reshape(f32[1088,4352]{1,0:T(8,128)} %fusion.51) | data formatting | bytes 37879808 | tf_op jit(solution)/shard_map/reshape;reshape | solution.py:58
  753.1 8.3 fusion.61
  761.5 24.4 %reshape_reshape.14 = f32[32,147968]{1,0:T(8,128)} reshape(f32[4352,1088]{1,0:T(8,128)} %fusion.61) | data formatting | bytes 37879808 | tf_op jit(solution)/shard_map/reshape;reshape | solution.py:58
  786.0 30.5 %pad_maximum_fusion = f32[32,296072]{1,0:T(8,128)} fusion(f32[32,136]{1,0:T(8,128)S(1)} %reshape.242, f32[32,147968]{1,0:T(8,128)} %reshape_reshape.15, f32[32,147968]{1,0:T(8,128)} %reshape_reshape.14), kind=kLoop, calls=%fused_computation.1 | loop fusion | flops 18948608 | bytes 75794432 | tf_op jit(solution)/shard_map/concatenate | solution.py:159
  826.4 16.9 fusion.96
  852.4 7.4 fusion.55
  860.0 14.6 reshape_reshape.12
  874.6 11.0 constant_dynamic-update-slice_fusion.1
  894.3 8.9 fusion.4
  904.2 795.2 %all-reduce.9.cloned.1.call-done = (f32[32,148240]{1,0:T(8,128)}, f32[32,296072]{1,0:T(8,128)}) async-done(((f32[32,148240]{1,0:T(8,128)}, f32[32,296072]{1,0:T(8,128)}), (f32[32,148240]{1,0:T(8,128)}, f32[32,296072]{1,0:T(8,128)})) %all-reduce.9.cloned.1.call-update) | async-done | bytes 56871952
  1705.8 10.0 dynamic-slice_reduce_fusion
  (149 shorter events, 88.4 us)
Async XLA Ops:
  7.2 8.4 copy-start.20
  7.2 12.5 copy-start.24
  7.2 12.8 copy-start.25
  7.2 13.0 copy-start.26
  7.2 71.0 %all-gather.11.cloned.1.call-start = ((), (), s32[]{:S(2)}) async-start(), calls=%async_computation.3 | async-start | bytes 4882944 | tf_op jit(solution)/shard_map/all_gather | solution.py:84
  8.9 55.1 %copy-start.23 = (s32[1,256]{1,0:T(1,128)S(1)}, s32[1,256]{1,0:T(1,128)}, u32[]{:S(2)}) copy-start(s32[1,256]{1,0:T(1,128)} %param.11) | copy-start | bytes 3076
  8.9 55.2 %copy-start = (bf16[1,128,1088]{1,2,0:T(8,128)(2,1)S(1)}, bf16[1,128,1088]{1,2,0:T(8,128)(2,1)}, u32[]{:S(2)}) copy-start(bf16[1,128,1088]{1,2,0:T(8,128)(2,1)} %param.10) | copy-start | bytes 835588
  9.0 174.1 %all-gather.9.cloned.1.call-start = ((), (), s32[]{:S(2)}) async-start(), calls=%async_computation.2 | async-start | bytes 14648832 | tf_op jit(solution)/shard_map/all_gather | solution.py:83
  11.0 327.3 %all-gather.15.cloned.1.call-start = ((), (), s32[]{:S(2)}) async-start(), calls=%async_computation.5 | async-start | bytes 19531776 | tf_op jit(solution)/shard_map/all_gather | solution.py:86
  15.5 490.9 %all-gather.13.cloned.1.call-start = ((), (), s32[]{:S(2)}) async-start(), calls=%async_computation.4 | async-start | bytes 19531776 | tf_op jit(solution)/shard_map/all_gather | solution.py:85
  19.7 823.7 %reduce-scatter.9.cloned.1.call-start = ((), (), s32[]{:S(2)}) async-start(), calls=%async_computation.7 | async-start | bytes 884736
  680.2 13.3 slice-start
  680.2 13.3 slice-start.1
  685.8 7.7 copy-start.1
  685.8 7.7 slice-start.2
  708.8 135.8 %reduce-scatter.7.cloned.1.call-start = ((), (), s32[]{:S(2)}) async-start(), calls=%async_computation.6 | async-start | bytes 884736
  710.5 16.2 copy-start.9
  728.9 24.2 %copy-start.2 = (f32[128,4352]{1,0:T(8,128)S(1)}, f32[128,4352]{1,0:T(8,128)}, u32[]{:S(2)}) copy-start(f32[128,4352]{1,0:T(8,128)} %copy-done.1) | copy-start | bytes 6684676
  729.0 24.2 %copy-start.18 = (bf16[1,128,1088]{1,2,0:T(8,128)(2,1)S(1)}, bf16[1,128,1088]{1,2,0:T(8,128)(2,1)}, u32[]{:S(2)}) copy-start(bf16[1,128,1088]{1,2,0:T(8,128)(2,1)} %param.19) | copy-start | bytes 835588
  785.9 30.6 %copy-start.15 = (bf16[17,64,128]{2,1,0:T(8,128)(2,1)S(1)}, bf16[17,64,128]{2,1,0:T(8,128)(2,1)}, u32[]{:S(2)}) copy-start(bf16[17,64,128]{2,1,0:T(8,128)(2,1)} %copy-done.14) | copy-start | bytes 835588
  786.0 913.5 %all-reduce.9.cloned.1.call-start = ((), (), s32[]{:S(2)}) async-start(), calls=%async_computation.8 | async-start | bytes 113803264
  786.0 30.5 %copy-start.6 = (f32[128,1088]{0,1:T(8,128)S(1)}, f32[128,1088]{0,1:T(8,128)}, u32[]{:S(2)}) copy-start(f32[128,1088]{0,1:T(8,128)} %copy-done.5) | copy-start | bytes 1671172
  894.3 8.9 copy-start.7
  894.3 8.9 copy-start.19
  (13 other events, 38.4 us)
Sparse Core Ops, SparseCore 0:
  11.5 66.7 all-gather.10
  81.7 101.3 all-gather.8
  186.6 122.6 all-gather.14
  312.6 122.4 all-gather.12
  708.9 6.4 reduce-scatter.8
  786.1 6.2 reduce-scatter.6
  893.7 805.6 all-reduce.8
where the time goes:
time: 1730 us
  waiting for transfers between devices  858 us (50%)
  other arithmetic  528 us (31%)
  local copies, waits for them, and re-layouts  173 us (10%)
  matrix products  103 us (6%)
  blocking collectives  48 us (3%)
    unnamed x10, waiting for transfers between devices  795 us
    all_gather x1, other arithmetic, per_device(): lax.all_gather(w_fc, ('dp', 'seq'), axis=0, tiled=True)  157 us
    all_gather x1, other arithmetic, per_device(): lax.all_gather(w_proj, ('dp', 'seq'), axis=0, tiled=True)  156 us
    all_gather x1, other arithmetic, per_device(): lax.all_gather(w_attn, ('dp', 'seq'), axis=0, tiled=True)  130 us
    another operation x4, local copies, waits for them, and re-layouts, shard_rows(): return flat_term(left, right).reshape(count, shard)  69.7 us
    all_gather x1, other arithmetic, per_device(): lax.all_gather(w_out, ('dp', 'seq'), axis=0, tiled=True)  50.9 us
    all_gather x1, waiting for transfers between devices, per_device(): lax.all_gather(w_attn, ('dp', 'seq'), axis=0, tiled=True)  49.9 us
    unnamed x1, blocking collectives  43.5 us
  transfers between devices with their start and end apart: 7, of which 3 were waited for; matrix products, arithmetic and copies ran while one was open for 31% of the time, Pallas kernels for 0%

commit v1 on v0

v1 whole, which is shorter than its diff:
```python
import jax
import jax.numpy as jnp
from jax import lax
from jax.sharding import PartitionSpec as P

HD = 64
FF = 4352


GELU_C = 0.7978845608028654
NORM_EPS = 1e-05


def gelu_parts(inputs):
    tanh_value = jnp.tanh(GELU_C * (inputs + 0.044715 * inputs * inputs * inputs))
    value = 0.5 * inputs * (1.0 + tanh_value)
    slope = 0.5 * (1.0 + tanh_value) + 0.5 * inputs * (1.0 - tanh_value * tanh_value) * GELU_C * (
        1.0 + 3.0 * 0.044715 * inputs * inputs
    )
    return (value, slope)


def layer_norm(inputs, gains, offsets):
    average = jnp.mean(inputs, axis=-1, keepdims=True)
    centred = inputs - average
    inv_std = lax.rsqrt(jnp.mean(centred * centred, axis=-1, keepdims=True) + NORM_EPS)
    x_hat = centred * inv_std
    return (x_hat * gains + offsets, x_hat, inv_std)


def norm_back(grad_out, x_hat, inv_std, gains):
    grad_hat = grad_out * gains
    grad_in = inv_std * (
        grad_hat
        - jnp.mean(grad_hat, axis=-1, keepdims=True)
        - x_hat * jnp.mean(grad_hat * x_hat, axis=-1, keepdims=True)
    )
    return (grad_in, jnp.sum(grad_out * x_hat, axis=0), jnp.sum(grad_out, axis=0))


def score_block(queries, key_rows, allowed):
    scores = jnp.einsum(
        "qhd,khd->hqk", queries, key_rows, preferred_element_type=jnp.float32
    ) * HD ** (-0.5)
    return jnp.where(allowed[None], scores, -1e30)


def outer_sum(left, right):
    return jnp.einsum("na,nb->ab", left, right, preferred_element_type=jnp.float32)


AXES = ("dp", "seq")


def shard_height(shard, columns):
    size = shard.shape[0]
    return size // columns if size % columns == 0 else 0


def padded(height):
    return -(-height // 8) * 8


def gather_rows(shard, columns, extra=None):
    height = shard_height(shard, columns)
    if not height:
        return lax.all_gather(shard, AXES, axis=0, tiled=True).reshape(-1, columns)
    block = shard.reshape(height, columns)
    room = padded(height) - height
    if extra is not None:
        row = jnp.pad(extra, (0, columns - extra.shape[0]))[None]
        block = jnp.concatenate([block, row], axis=0)
        room -= 1
    if room:
        block = jnp.pad(block, ((0, room), (0, 0)))
    return lax.all_gather(block, AXES, axis=0, tiled=True)


def spread(acts, height):
    room = padded(height) - height
    if not room:
        return acts
    tokens = acts.shape[0]
    parts = acts.reshape(tokens, -1, height)
    return jnp.pad(parts, ((0, 0), (0, 0), (0, room))).reshape(tokens, -1)


def unspread(acts, height):
    if padded(height) == height:
        return acts
    tokens = acts.shape[0]
    return acts.reshape(tokens, -1, padded(height))[:, :, :height].reshape(tokens, -1)


def scatter_rows(blocks, height):
    count = lax.axis_size(AXES)
    sums = lax.psum_scatter(
        blocks.astype(jnp.bfloat16).reshape(count, -1, blocks.shape[-1]),
        AXES,
        scatter_dimension=0,
        tiled=True,
    )[0]
    return sums.astype(jnp.float32)


def scatter_flat(block, shard):
    count = lax.axis_size(AXES)
    return lax.psum_scatter(
        block.reshape(count, shard), AXES, scatter_dimension=0, tiled=True
    )[0]


def per_device(
    layer_input,
    segments,
    w_attn,
    w_out,
    w_fc,
    w_proj,
    norm_params,
    lin_bias,
    fc_bias,
    out_cotangent,
):
    tokens = layer_input.shape[1]
    width = layer_input.shape[2]
    heads = width // HD
    place = lax.axis_index("seq")
    first = place * tokens
    small = norm_params.shape[0]
    height = shard_height(w_attn, 3 * width)
    height = height if shard_height(w_out, width) == height == shard_height(w_fc, FF) else 0
    down_height = shard_height(w_proj, width)
    own_small = jnp.concatenate([norm_params, lin_bias, fc_bias])
    packed = height and padded(height) > height and own_small.shape[0] <= width
    w_qkv = gather_rows(w_attn, 3 * width)
    w_o = gather_rows(w_out, width, own_small if packed else None)
    w_up = gather_rows(w_fc, FF)
    w_down = gather_rows(w_proj, width)
    if packed:
        smalls = w_o.reshape(-1, padded(height), width)[:, height, : 3 * small]
    else:
        smalls = lax.all_gather(own_small, AXES, axis=0)
    smalls = smalls.astype(jnp.float32).reshape(-1, 3, small)
    norms = smalls[:, 0].reshape(4, width)
    biases = smalls[:, 1].reshape(4, width)
    up_bias = smalls[:, 2].reshape(FF)
    inputs_f = layer_input[0].astype(jnp.float32)
    normed1, x_hat1, inv_std1 = layer_norm(inputs_f, norms[0], norms[1])
    act_in1 = normed1.astype(jnp.bfloat16)
    act_rows1 = spread(act_in1, height)
    projected = jnp.dot(act_rows1, w_qkv, preferred_element_type=jnp.float32)
    queries = (projected[:, :width] + biases[0]).astype(jnp.bfloat16)
    own_keys = projected[:, width : 2 * width].astype(jnp.bfloat16)
    own_values = (projected[:, 2 * width :] + biases[1]).astype(jnp.bfloat16)
    key_rows, value_rows = (
        lax.all_gather(own_keys, "seq", axis=0, tiled=True),
        lax.all_gather(own_values, "seq", axis=0, tiled=True),
    )
    key_count = key_rows.shape[0]
    key_pos = jnp.arange(key_count)
    query_pos = first + jnp.arange(tokens)
    padded_seg = jnp.concatenate([jnp.full((tokens,), -1, jnp.int32), segments[0]])
    key_seg = lax.dynamic_slice_in_dim(padded_seg, tokens, key_count)
    query_seg = lax.dynamic_slice_in_dim(segments[0], first, tokens)
    allowed = (key_pos[None, :] <= query_pos[:, None]) & (key_seg[None, :] == query_seg[:, None])
    q_heads = queries.reshape(tokens, heads, HD)
    k_heads = key_rows.reshape(key_count, heads, HD)
    v_heads = value_rows.reshape(key_count, heads, HD)
    scores = score_block(q_heads, k_heads, allowed)
    top_score = jnp.max(scores, axis=-1, keepdims=True)
    log_total = top_score + jnp.log(jnp.sum(jnp.exp(scores - top_score), axis=-1, keepdims=True))
    attn_probs = jnp.exp(scores - log_total).astype(jnp.bfloat16)
    attended = jnp.einsum("hqk,khd->qhd", attn_probs, v_heads, preferred_element_type=jnp.float32)
    attended = attended.reshape(tokens, width).astype(jnp.bfloat16)
    attended_rows = spread(attended, height)
    resid = inputs_f + jnp.dot(attended_rows, w_o, preferred_element_type=jnp.float32) + biases[2]
    normed2, x_hat2, inv_std2 = layer_norm(resid, norms[2], norms[3])
    act_in2 = normed2.astype(jnp.bfloat16)
    act_rows2 = spread(act_in2, height)
    hidden_pre = jnp.dot(act_rows2, w_up, preferred_element_type=jnp.float32) + up_bias
    hidden_act, hidden_slope = gelu_parts(hidden_pre)
    hidden_b = hidden_act.astype(jnp.bfloat16)
    hidden_rows = spread(hidden_b, down_height)
    result = (
        resid + jnp.dot(hidden_rows, w_down, preferred_element_type=jnp.float32) + biases[3]
    ).astype(jnp.bfloat16)
    cotangent = out_cotangent[0]
    grad_out = cotangent.astype(jnp.float32)
    grad_bp = jnp.sum(grad_out, axis=0)
    grad_hidden = (
        unspread(
            jnp.einsum("nd,fd->nf", cotangent, w_down, preferred_element_type=jnp.float32),
            down_height,
        )
        * hidden_slope
    )
    grad_hidden_b = grad_hidden.astype(jnp.bfloat16)
    grad_up_bias = jnp.sum(grad_hidden, axis=0)
    grad_down = outer_sum(hidden_rows, cotangent)
    if down_height:
        proj_sums = scatter_rows(grad_down, down_height)[:down_height].reshape(-1)
    else:
        proj_sums = scatter_flat(grad_down, w_proj.shape[0])
    grad_up = outer_sum(act_rows2, grad_hidden_b)
    if height:
        fc_sums = scatter_rows(grad_up, height)[:height].reshape(-1)
    else:
        fc_sums = scatter_flat(grad_up, w_fc.shape[0])
    grad_norm2 = unspread(
        jnp.einsum("nf,df->nd", grad_hidden_b, w_up, preferred_element_type=jnp.float32), height
    )
    grad_resid_n, grad_g2, grad_b2 = norm_back(grad_norm2, x_hat2, inv_std2, norms[2])
    grad_resid = grad_out + grad_resid_n
    grad_resid_b = grad_resid.astype(jnp.bfloat16)
    grad_bo = jnp.sum(grad_resid, axis=0)
    grad_att = unspread(
        jnp.einsum(
            "ne,de->nd", grad_resid_b, w_o, preferred_element_type=jnp.float32
        ).astype(jnp.bfloat16),
        height,
    )
    grad_att_heads = grad_att.reshape(tokens, heads, HD)
    probs_full = jnp.exp(score_block(q_heads, k_heads, allowed) - log_total)
    probs_b = probs_full.astype(jnp.bfloat16)
    grad_probs = jnp.einsum(
        "qhd,khd->hqk", grad_att_heads, v_heads, preferred_element_type=jnp.float32
    )
    delta = jnp.sum(probs_full * grad_probs, axis=-1, keepdims=True)
    grad_scores = (probs_full * (grad_probs - delta) * HD ** (-0.5)).astype(jnp.bfloat16)
    grad_q = jnp.einsum(
        "hqk,khd->qhd", grad_scores, k_heads, preferred_element_type=jnp.float32
    ).reshape(tokens, width)
    grad_k_all = jnp.einsum(
        "hqk,qhd->khd", grad_scores, q_heads, preferred_element_type=jnp.float32
    ).reshape(key_count, width)
    grad_v_all = jnp.einsum(
        "hqk,qhd->khd", probs_b, grad_att_heads, preferred_element_type=jnp.float32
    ).reshape(key_count, width)
    grad_k, grad_v = (
        lax.psum_scatter(
            grad_k_all.astype(jnp.bfloat16), "seq", scatter_dimension=0, tiled=True
        ).astype(jnp.float32),
        lax.psum_scatter(
            grad_v_all.astype(jnp.bfloat16), "seq", scatter_dimension=0, tiled=True
        ).astype(jnp.float32),
    )
    grad_proj_b = jnp.concatenate([grad_q, grad_k, grad_v], axis=1).astype(jnp.bfloat16)
    grad_norm1 = unspread(
        jnp.einsum("ne,de->nd", grad_proj_b, w_qkv, preferred_element_type=jnp.float32), height
    )
    grad_in_n, grad_g1, grad_b1 = norm_back(grad_norm1, x_hat1, inv_std1, norms[0])
    grad_input = grad_resid + grad_in_n
    norm_terms = jnp.concatenate([grad_g1, grad_b1, grad_g2, grad_b2])
    bias_terms = jnp.concatenate(
        [jnp.sum(grad_q, axis=0), jnp.sum(grad_v, axis=0), grad_bo, grad_bp]
    )
    small_terms = jnp.concatenate(
        [term.reshape(-1, 1, small) for term in (norm_terms, bias_terms, grad_up_bias)], axis=1
    )
    grad_attn = outer_sum(act_rows1, grad_proj_b)
    grad_wo = outer_sum(attended_rows, grad_resid_b)
    if height:
        joined = jnp.concatenate(
            [grad_attn.astype(jnp.bfloat16), grad_wo.astype(jnp.bfloat16)], axis=1
        )
        if packed:
            blocks = joined.reshape(-1, padded(height), 4 * width)
            row = small_terms.astype(jnp.bfloat16).reshape(-1, 1, 3 * small)
            row = jnp.pad(row, ((0, 0), (height, padded(height) - height - 1), (0, width * 4 - 3 * small)))
            joined = (blocks + row).reshape(joined.shape)
        sums = scatter_rows(joined, height)
        qkv_sums = sums[:height, : 3 * width].reshape(-1)
        out_sums = sums[:height, 3 * width :].reshape(-1)
    else:
        qkv_sums = scatter_flat(grad_attn, w_attn.shape[0])
        out_sums = scatter_flat(grad_wo, w_out.shape[0])
    if packed:
        small_sums = sums[height, : 3 * small].reshape(3, small)
    else:
        small_sums = lax.psum_scatter(small_terms, AXES, scatter_dimension=0, tiled=True)[0]
    norm_sums, bias_sums, fcb_sums = small_sums[0], small_sums[1], small_sums[2]
    return (
        result[None],
        grad_input[None],
        qkv_sums,
        out_sums,
        fc_sums,
        proj_sums,
        norm_sums,
        bias_sums,
        fcb_sums,
    )


def solution(mesh):
    return jax.shard_map(
        per_device,
        mesh=mesh,
        in_specs=(
            P("dp", "seq", None),
            P("dp", None),
            P(("dp", "seq")),
            P(("dp", "seq")),
            P(("dp", "seq")),
            P(("dp", "seq")),
            P(("dp", "seq")),
            P(("dp", "seq")),
            P(("dp", "seq")),
            P("dp", "seq", None),
        ),
        out_specs=(
            P("dp", "seq", None),
            P("dp", "seq", None),
            P(("dp", "seq")),
            P(("dp", "seq")),
            P(("dp", "seq")),
            P(("dp", "seq")),
            P(("dp", "seq")),
            P(("dp", "seq")),
            P(("dp", "seq")),
        ),
        check_vma=False,
    )
```

time: 1730 us -> 859 us (0.50)
  other arithmetic: 528 us -> 33.5 us
  waiting for transfers between devices: 858 us -> 628 us
  local copies, waits for them, and re-layouts: 173 us -> 68.1 us
  blocking collectives: 48 us -> 4.63 us
    unnamed x10 -> x12, waiting for transfers between devices: 795 us -> 45.1 us
    all_gather x4 -> x0, other arithmetic: 494 us -> none  [the longest x1 157 us: per_device(): lax.all_gather(w_fc, ('dp', 'seq'), axis=0, tiled=True)]
    reduce_scatter x0 -> x2, waiting for transfers between devices: none -> 307 us  [scatter_rows(): lax.psum_scatter(blocks.astype(jnp.bfloat16).reshape(count, -1, blocks.sh...]
    all_gather x4, waiting for transfers between devices: 62.9 us -> 275 us  [gather_rows(): return lax.all_gather(block, AXES, axis=0, tiled=True)]
    another operation x4 -> x1, local copies, waits for them, and re-layouts: 69.7 us -> 0.09 us  [per_device(): grad_att_heads = grad_att.reshape(tokens, heads, HD)]
    unnamed x1 -> x0, blocking collectives: 43.5 us -> none
    reshape x5 -> x11, local copies, waits for them, and re-layouts: 42.8 us -> 12.1 us  [the longest x4 4.51 us: gather_rows(): block = shard.reshape(height, columns)]
    unnamed x77 -> x96, local copies, waits for them, and re-layouts: 38.7 us -> 12.9 us
  transfers between devices with their start and end apart: 7 -> 9, of which waited for: 3 -> 7; matrix products, arithmetic and copies ran while one was open for 31% -> 19% of each run, Pallas kernels for 0% -> 0%
where the time goes in v1:
time: 859 us; the launch traced here: 851 us
  waiting for transfers between devices  628 us (73%)
  matrix products  102 us (12%)
  local copies, waits for them, and re-layouts  68.1 us (8%)
  other arithmetic  33.5 us (4%)
  between operations  14.7 us (2%)
    reduce_scatter x2, waiting for transfers between devices, scatter_rows(): lax.psum_scatter(blocks.astype(jnp.bfloat16).reshape(count, -1, blocks.sh...  307 us
    all_gather x4, waiting for transfers between devices, gather_rows(): return lax.all_gather(block, AXES, axis=0, tiled=True)  275 us
    unnamed x12, waiting for transfers between devices  45.1 us
    dot_general x4, matrix products, outer_sum(): jnp.einsum('na,nb->ab', left, right, preferred_element_type=jnp.float32)  17.9 us
    dot_general x1, matrix products, per_device(): jnp.einsum('hqk,khd->qhd', grad_scores, k_heads, preferred_element_type=j...  17.3 us
  transfers between devices with their start and end apart: 9, of which 7 were waited for; matrix products, arithmetic and copies ran while one was open for 19% of the time, Pallas kernels for 0%

profile of v1, /device:TPU:0, one launch (start us, length us, event | category | flops | bytes accessed | tf_op | source)
XLA Modules:
  0.0 851.4 jit_solution(4152328101037689601)
XLA Ops:
  15.6 57.2 %all-gather.5.cloned.1.call-done = bf16[1280,1088]{1,0:T(8,128)(2,1)} async-done(((bf16[40,1088]{1,0:T(8,128)(2,1)}), bf16[1280,1088]{1,0:T(8,128)(2,1)}) %all-gather.5.cloned.1.call-update) | async-done | bytes 2785296 | tf_op jit(solution)/shard_map/all_gather | solution.py:76
  79.1 73.6 %all-gather.7.cloned.1.call-done = bf16[1280,3264]{1,0:T(8,128)(2,1)} async-done(((bf16[40,3264]{1,0:T(8,128)(2,1)}), bf16[1280,3264]{1,0:T(8,128)(2,1)}) %all-gather.7.cloned.1.call-update) | async-done | bytes 8355856 | tf_op jit(solution)/shard_map/all_gather | solution.py:76
  152.7 6.9 fusion.75
  162.3 2.4 all_gather.21
  178.0 65.9 %all-gather.9.cloned.1.call-done = bf16[1280,4352]{1,0:T(8,128)(2,1)} async-done(((bf16[40,4352]{1,0:T(8,128)(2,1)}), bf16[1280,4352]{1,0:T(8,128)(2,1)}) %all-gather.9.cloned.1.call-update) | async-done | bytes 11141136 | tf_op jit(solution)/shard_map/all_gather | solution.py:76
  243.9 7.3 convolution_add_fusion
  251.2 78.8 %all-gather.11.cloned.1.call-done = bf16[4352,1088]{1,0:T(8,128)(2,1)} async-done(((bf16[136,1088]{1,0:T(8,128)(2,1)}), bf16[4352,1088]{1,0:T(8,128)(2,1)}) %all-gather.11.cloned.1.call-update) | async-done | bytes 9469968 | tf_op jit(solution)/shard_map/all_gather | solution.py:76
  330.0 8.2 fusion.74
  338.2 3.1 fusion.33
  353.7 2.4 convolution_convert_fusion.5
  359.1 16.9 %fusion.20 = bf16[17,64,256]{2,1,0:T(8,128)(2,1)} fusion(bf16[128,17,64]{0,2,1:T(8,128)(2,1)S(1)} %bitcast.109, f32[17,128,256]{2,1,0:T(8,128)} %fusion.76, f32[17,128,256]{2,1,0:T(8,128)} %copy-done.4, f32[17,128]{1,0:T(8,128)S(1)} %copy-done.37, pred[128,256]{1,0:T(8,128)(4,1)S(1)} %fusion.42), kind=kOutput, calls=%fused_computation.33 | convolution fusion | flops 77711744 | bytes 5333504 | tf_op jit(solution)/shard_map/hqk,qhd->khd/dot_general | solution.py:234
  378.2 6.3 convolution_convert_fusion
  384.5 13.9 %copy.42 = bf16[4352,1088]{1,0:T(8,128)(2,1)} copy(bf16[4352,1088]{0,1:T(8,128)(2,1)} %convolution_convert_fusion) | data formatting | bytes 18939904 | tf_op jit(solution)/shard_map/convert_element_type | solution.py:98
  399.7 5.9 convolution_convert_fusion.1
  406.8 17.3 %fusion.70 = (bf16[17,64]{1,0:T(8,128)(2,1)S(1)}, bf16[128,17,64]{0,2,1:T(8,128)(2,1)}) fusion(bf16[256,17,64]{0,2,1:T(8,128)(2,1)S(1)} %bitcast.104, f32[17,128,256]{2,1,0:T(8,128)} %fusion.76, f32[17,128]{1,0:T(8,128)S(1)} %copy-done.37, f32[17,128,256]{2,1,0:T(8,128)} %copy-done.4, pred[128,256]{1,0:T(8,128)(4,1)S(1)} %fusion.42), kind=kOutput, calls=%fused_computation.124 | convolution fusion | flops 77710656 | bytes 5335680 | tf_op jit(solution)/shard_map/hqk,khd->qhd/dot_general | solution.py:231
  430.1 3.6 convolution_convert_fusion.2
  433.8 5.0 pad_maximum_fusion
  438.7 15.0 %copy.39 = bf16[1280,4352]{1,0:T(8,128)(2,1)} copy(bf16[1280,4352]{0,1:T(8,128)(2,1)} %pad_maximum_fusion) | data formatting | bytes 22282240 | tf_op jit(solution)/shard_map/concatenate | solution.py:264
  453.9 5.9 fusion.35
  461.3 10.6 %pad_add_fusion = bf16[32,40,4352]{2,1,0:T(8,128)(2,1)} fusion(bf16[32,40,4352]{2,1,0:T(8,128)(2,1)} %bitcast.93, bf16[32,1,408]{2,1,0:T(2,128)(2,1)S(1)} %convert_element_type.186), kind=kLoop, calls=%fused_computation.5 | loop fusion | flops 22282240 | bytes 22308352 | tf_op jit(solution)/shard_map/add | solution.py:271
  473.6 8.4 fusion.4
  485.2 45.0 %reduce-scatter.20.cloned.1.call-done = bf16[1,136,1088]{2,1,0:T(8,128)(2,1)} async-done(((bf16[32,136,1088]{2,1,0:T(8,128)(2,1)}), bf16[1,136,1088]{2,1,0:T(8,128)(2,1)}) %reduce-scatter.20.cloned.1.call-update) | async-done | bytes 295952
  532.3 154.9 %reduce-scatter.14.cloned.1.call-done = bf16[1,40,4352]{2,1,0:T(8,128)(2,1)} async-done(((bf16[32,40,4352]{2,1,0:T(8,128)(2,1)}), bf16[1,40,4352]{2,1,0:T(8,128)(2,1)}) %reduce-scatter.14.cloned.1.call-update) | async-done | bytes 348176 | tf_op jit(solution)/shard_map/reduce_scatter | solution.py:97
  689.1 152.1 %reduce-scatter.12.cloned.1.call-done = bf16[1,40,4352]{2,1,0:T(8,128)(2,1)} async-done(((bf16[32,40,4352]{2,1,0:T(8,128)(2,1)}), bf16[1,40,4352]{2,1,0:T(8,128)(2,1)}) %reduce-scatter.12.cloned.1.call-update) | async-done | bytes 348176 | tf_op jit(solution)/shard_map/reduce_scatter | solution.py:97
  (204 shorter events, 70.4 us)
Async XLA Ops:
  7.2 7.9 copy-start.9
  7.2 65.6 %all-gather.5.cloned.1.call-start = ((), (), s32[]{:S(2)}) async-start(), calls=%async_computation.5 | async-start | bytes 3041280 | tf_op jit(solution)/shard_map/all_gather | solution.py:76
  9.8 142.9 %all-gather.7.cloned.1.call-start = ((), (), s32[]{:S(2)}) async-start(), calls=%async_computation.6 | async-start | bytes 8785920 | tf_op jit(solution)/shard_map/all_gather | solution.py:76
  11.8 232.2 %all-gather.9.cloned.1.call-start = ((), (), s32[]{:S(2)}) async-start(), calls=%async_computation.7 | async-start | bytes 11489280 | tf_op jit(solution)/shard_map/all_gather | solution.py:76
  13.9 316.0 %all-gather.11.cloned.1.call-start = ((), (), s32[]{:S(2)}) async-start(), calls=%async_computation.8 | async-start | bytes 10340352 | tf_op jit(solution)/shard_map/all_gather | solution.py:76
  15.0 411.5 %reduce-scatter.18.cloned.1.call-start = ((), (), s32[]{:S(2)}) async-start(), calls=%async_computation.12 | async-start | bytes 884736
  15.1 144.5 %copy-start.10 = (f32[128,32,34]{0,2,1:T(8,128)}, f32[128,32,34]{0,2,1:T(8,128)S(1)}, u32[]{:S(2)}) copy-start(f32[128,32,34]{0,2,1:T(8,128)S(1)} %reshape.374) | copy-start | bytes 1671172
  15.4 61.6 %copy-start.39 = (f32[128]{0:T(128)}, f32[128]{0:T(128)S(1)}, u32[]{:S(2)}) copy-start(f32[128]{0:T(128)S(1)} %broadcast_multiply_fusion.5) | copy-start | bytes 1540
  15.5 144.1 %copy-start.42 = (f32[128]{0:T(128)}, f32[128]{0:T(128)S(1)}, u32[]{:S(2)}) copy-start(f32[128]{0:T(128)S(1)} %add_rsqrt_fusion.1) | copy-start | bytes 1540
  77.4 82.2 %copy-start.14 = (bf16[128,32,40]{0,2,1:T(8,128)(2,1)}, bf16[128,32,40]{0,2,1:T(8,128)(2,1)S(1)}, u32[]{:S(2)}) copy-start(bf16[128,32,40]{0,2,1:T(8,128)(2,1)S(1)} %pad.32) | copy-start | bytes 983044
  329.9 8.2 copy-start
  357.2 71.1 %reduce-scatter.16.cloned.1.call-start = ((), (), s32[]{:S(2)}) async-start(), calls=%async_computation.11 | async-start | bytes 884736
  359.1 19.1 %copy-start.2 = (f32[128,4352]{1,0:T(8,128)S(1)}, f32[128,4352]{1,0:T(8,128)}, u32[]{:S(2)}) copy-start(f32[128,4352]{1,0:T(8,128)} %convolution_add_fusion) | copy-start | bytes 6684676
  359.1 19.1 %copy-start.13 = (bf16[1,128,1088]{1,2,0:T(8,128)(2,1)S(1)}, bf16[1,128,1088]{1,2,0:T(8,128)(2,1)}, u32[]{:S(2)}) copy-start(bf16[1,128,1088]{1,2,0:T(8,128)(2,1)} %param.19) | copy-start | bytes 835588
  378.1 152.0 %reduce-scatter.20.cloned.1.call-start = ((), (), s32[]{:S(2)}) async-start(), calls=%async_computation.13 | async-start | bytes 10340352
  398.4 288.7 %reduce-scatter.14.cloned.1.call-start = ((), (), s32[]{:S(2)}) async-start(), calls=%async_computation.10 | async-start | bytes 11489280 | tf_op jit(solution)/shard_map/reduce_scatter | solution.py:97
  405.7 435.5 %reduce-scatter.12.cloned.1.call-start = ((), (), s32[]{:S(2)}) async-start(), calls=%async_computation.9 | async-start | bytes 11489280 | tf_op jit(solution)/shard_map/reduce_scatter | solution.py:97
  406.8 17.4 %copy-start.31 = (bf16[32,34]{1,0:T(8,128)(2,1)S(1)}, bf16[32,34]{1,0:T(8,128)(2,1)}, u32[]{:S(2)}) copy-start(bf16[32,34]{1,0:T(8,128)(2,1)} %get-tuple-element.15) | copy-start | bytes 6532
  406.8 17.5 %copy-start.34 = (bf16[1088]{0:T(1024)(128)(2,1)S(1)}, bf16[1088]{0:T(1024)(128)(2,1)}, u32[]{:S(2)}) copy-start(bf16[1088]{0:T(1024)(128)(2,1)} %get-tuple-element.11) | copy-start | bytes 6532
  438.7 15.0 %copy-start.20 = (bf16[128,1088]{1,0:T(8,128)(2,1)S(1)}, bf16[128,1088]{1,0:T(8,128)(2,1)}, u32[]{:S(2)}) copy-start(bf16[128,1088]{1,0:T(8,128)(2,1)} %reduce-scatter.18.cloned.1.call-done) | copy-start | bytes 835588
  438.7 15.1 %copy-start.23 = (bf16[128,1088]{0,1:T(8,128)(2,1)S(1)}, bf16[128,1088]{0,1:T(8,128)(2,1)}, u32[]{:S(2)}) copy-start(bf16[128,1088]{0,1:T(8,128)(2,1)} %copy.48) | copy-start | bytes 835588
  438.7 15.2 %copy-start.24 = (bf16[128,1088]{0,1:T(8,128)(2,1)S(1)}, bf16[128,1088]{0,1:T(8,128)(2,1)}, u32[]{:S(2)}) copy-start(bf16[128,1088]{0,1:T(8,128)(2,1)} %copy.46) | copy-start | bytes 835588
  438.7 15.2 %copy-start.26 = (bf16[128,17,64]{0,2,1:T(8,128)(2,1)S(1)}, bf16[128,17,64]{0,2,1:T(8,128)(2,1)}, u32[]{:S(2)}) copy-start(bf16[128,17,64]{0,2,1:T(8,128)(2,1)} %get-tuple-element.35) | copy-start | bytes 835588
  473.6 9.6 %copy-start.6 = (f32[128,1088]{0,1:T(8,128)S(1)}, f32[128,1088]{0,1:T(8,128)}, u32[]{:S(2)}) copy-start(f32[128,1088]{0,1:T(8,128)} %copy-done.5) | copy-start | bytes 1671172
  (31 other events, 83.0 us)
Sparse Core Ops, SparseCore 0:
  11.5 61.2 all-gather.4
  76.2 76.4 all-gather.6
  156.1 87.7 all-gather.8
  247.3 82.6 all-gather.10
  357.3 6.5 reduce-scatter.17
  378.3 6.3 reduce-scatter.15
  398.6 131.5 reduce-scatter.19
  532.5 154.6 reduce-scatter.13
  689.5 151.6 reduce-scatter.11

commit v2 on v1

--- a/solution.py
+++ b/solution.py
@@ -57,12 +57,16 @@
     return size // columns if size % columns == 0 else 0
 
 
+def tile_height(shard, columns):
+    height = shard_height(shard, columns)
+    return 0 if height % 8 else height
+
+
 def padded(height):
     return -(-height // 8) * 8
 
 
-def gather_rows(shard, columns, extra=None):
-    height = shard_height(shard, columns)
+def gather_rows(shard, columns, height, extra=None):
     if not height:
         return lax.all_gather(shard, AXES, axis=0, tiled=True).reshape(-1, columns)
     block = shard.reshape(height, columns)
@@ -108,6 +112,17 @@
     return lax.psum_scatter(
         block.reshape(count, shard), AXES, scatter_dimension=0, tiled=True
     )[0]
+
+
+def own_half_sum(terms, place, tokens):
+    if lax.axis_size("seq") != 2:
+        return lax.psum_scatter(
+            terms.astype(jnp.bfloat16), "seq", scatter_dimension=0, tiled=True
+        ).astype(jnp.float32)
+    own = lax.dynamic_slice_in_dim(terms, place * tokens, tokens)
+    other = lax.dynamic_slice_in_dim(terms, (1 - place) * tokens, tokens)
+    came = lax.ppermute(other.astype(jnp.bfloat16), "seq", [(0, 1), (1, 0)])
+    return own + came.astype(jnp.float32)
 
 
 def per_device(
@@ -130,13 +145,28 @@
     small = norm_params.shape[0]
     height = shard_height(w_attn, 3 * width)
     height = height if shard_height(w_out, width) == height == shard_height(w_fc, FF) else 0
-    down_height = shard_height(w_proj, width)
+    down_height = tile_height(w_proj, width)
     own_small = jnp.concatenate([norm_params, lin_bias, fc_bias])
     packed = height and padded(height) > height and own_small.shape[0] <= width
-    w_qkv = gather_rows(w_attn, 3 * width)
-    w_o = gather_rows(w_out, width, own_small if packed else None)
-    w_up = gather_rows(w_fc, FF)
-    w_down = gather_rows(w_proj, width)
+    if height:
+        lanes = -(-width // 128) * 128
+        joined_shard = jnp.concatenate(
+            [
+                jnp.pad(w_out.reshape(height, width), ((0, 0), (0, lanes - width))),
+                w_attn.reshape(height, 3 * width),
+            ],
+            axis=1,
+        ).reshape(-1)
+        joined_w = gather_rows(
+            joined_shard, lanes + 3 * width, height, own_small if packed else None
+        )
+        w_o = joined_w[:, :width]
+        w_qkv = joined_w[:, lanes:]
+    else:
+        w_qkv = gather_rows(w_attn, 3 * width, 0)
+        w_o = gather_rows(w_out, width, 0)
+    w_up = gather_rows(w_fc, FF, height)
+    w_down = gather_rows(w_proj, width, down_height)
     if packed:
         smalls = w_o.reshape(-1, padded(height), width)[:, height, : 3 * small]
     else:
@@ -196,8 +226,12 @@
         * hidden_slope
     )
     grad_hidden_b = grad_hidden.astype(jnp.bfloat16)
+    grad_down = outer_sum(hidden_rows, cotangent)
+    if down_height:
+        grad_hidden_b, grad_down = lax.optimization_barrier(
+            (grad_hidden_b, grad_down.astype(jnp.bfloat16))
+        )
     grad_up_bias = jnp.sum(grad_hidden, axis=0)
-    grad_down = outer_sum(hidden_rows, cotangent)
     if down_height:
         proj_sums = scatter_rows(grad_down, down_height)[:down_height].reshape(-1)
     else:
@@ -237,14 +271,8 @@
     grad_v_all = jnp.einsum(
         "hqk,qhd->khd", probs_b, grad_att_heads, preferred_element_type=jnp.float32
     ).reshape(key_count, width)
-    grad_k, grad_v = (
-        lax.psum_scatter(
-            grad_k_all.astype(jnp.bfloat16), "seq", scatter_dimension=0, tiled=True
-        ).astype(jnp.float32),
-        lax.psum_scatter(
-            grad_v_all.astype(jnp.bfloat16), "seq", scatter_dimension=0, tiled=True
-        ).astype(jnp.float32),
-    )
+    grad_k = own_half_sum(grad_k_all, place, tokens)
+    grad_v = own_half_sum(grad_v_all, place, tokens)
     grad_proj_b = jnp.concatenate([grad_q, grad_k, grad_v], axis=1).astype(jnp.bfloat16)
     grad_norm1 = unspread(
         jnp.einsum("ne,de->nd", grad_proj_b, w_qkv, preferred_element_type=jnp.float32), height

time: 859 us -> 764 us (0.89)
  waiting for transfers between devices: 628 us -> 531 us
    all_gather x4 -> x3, waiting for transfers between devices: 275 us -> 223 us  [gather_rows(): return lax.all_gather(block, AXES, axis=0, tiled=True)]
    unnamed x12 -> x7, waiting for transfers between devices: 45.1 us -> 0.88 us
    optimization_barrier x0 -> x1, local copies, waits for them, and re-layouts: none -> 13.9 us  [per_device(): lax.optimization_barrier((grad_hidden_b, grad_down.astype(jnp.bfloat16)))]
    convert_element_type x1 -> x2, local copies, waits for them, and re-layouts: 13.9 us -> 2.52 us  [own_half_sum(): came = lax.ppermute(other.astype(jnp.bfloat16), 'seq', [(0, 1), (1, 0)])]
  transfers between devices with their start and end apart: 9 -> 8, of which waited for: 7 -> 6; matrix products, arithmetic and copies ran while one was open for 19% -> 22% of each run, Pallas kernels for 0% -> 0%
where the time goes in v2:
time: 764 us; the launch traced here: 757 us
  waiting for transfers between devices  531 us (70%)
  matrix products  107 us (14%)
  local copies, waits for them, and re-layouts  65.4 us (9%)
  other arithmetic  33.2 us (4%)
  between operations  14.9 us (2%)
    reduce_scatter x2, waiting for transfers between devices, scatter_rows(): lax.psum_scatter(blocks.astype(jnp.bfloat16).reshape(count, -1, blocks.sh...  307 us
    all_gather x3, waiting for transfers between devices, gather_rows(): return lax.all_gather(block, AXES, axis=0, tiled=True)  223 us
    dot_general x4, matrix products, outer_sum(): jnp.einsum('na,nb->ab', left, right, preferred_element_type=jnp.float32)  21.1 us
    dot_general x1, matrix products, per_device(): jnp.einsum('hqk,khd->qhd', grad_scores, k_heads, preferred_element_type=j...  15.6 us
    dot_general x1, matrix products, per_device(): jnp.einsum('hqk,qhd->khd', grad_scores, q_heads, preferred_element_type=j...  15.5 us
  transfers between devices with their start and end apart: 8, of which 6 were waited for; matrix products, arithmetic and copies ran while one was open for 22% of the time, Pallas kernels for 0%

profile of v2, /device:TPU:0, one launch (start us, length us, event | category | flops | bytes accessed | tf_op | source)
XLA Modules:
  0.0 757.0 jit_solution(18191499548203572886)
XLA Ops:
  14.1 90.5 %all-gather.4.cloned.1.call-done = bf16[1280,4416]{1,0:T(8,128)(2,1)} async-done(((bf16[40,4416]{1,0:T(8,128)(2,1)}), bf16[1280,4416]{1,0:T(8,128)(2,1)}) %all-gather.4.cloned.1.call-update) | async-done | bytes 11304976 | tf_op jit(solution)/shard_map/all_gather | solution.py:80
  108.6 6.8 fusion.3
  118.1 2.4 all_gather.17
  126.0 3.1 fusion.77
  135.0 60.7 %all-gather.6.cloned.1.call-done = bf16[1280,4352]{1,0:T(8,128)(2,1)} async-done(((bf16[40,4352]{1,0:T(8,128)(2,1)}), bf16[1280,4352]{1,0:T(8,128)(2,1)}) %all-gather.6.cloned.1.call-update) | async-done | bytes 11141136 | tf_op jit(solution)/shard_map/all_gather | solution.py:80
  195.7 6.0 convolution_add_fusion
  203.1 6.2 convolution_convert_fusion
  209.3 72.0 %all-gather.8.cloned.1.call-done = bf16[4352,1088]{1,0:T(8,128)(2,1)} async-done(((bf16[136,1088]{1,0:T(8,128)(2,1)}), bf16[4352,1088]{1,0:T(8,128)(2,1)}) %all-gather.8.cloned.1.call-update) | async-done | bytes 9469968 | tf_op jit(solution)/shard_map/all_gather | solution.py:80
  281.3 8.5 %fusion.74 = (bf16[4352]{0:T(1024)(128)(2,1)S(1)}, bf16[128,4352]{1,0:T(8,128)(2,1)}) fusion(f32[128,4352]{1,0:T(8,128)} %copy-done.1, bf16[4352,1088]{1,0:T(8,128)(2,1)} %all-gather.8.cloned.1.call-done, bf16[1,128,1088]{1,2,0:T(8,128)(2,1)} %param.19), kind=kOutput, calls=%fused_computation.134 | convolution fusion | flops 1223290624 | bytes 13099520 | tf_op jit(solution)/shard_map/nd,fd->nf/dot_general | solution.py:223
  289.8 13.9 %copy.42 = bf16[4352,1088]{1,0:T(8,128)(2,1)} copy(bf16[4352,1088]{0,1:T(8,128)(2,1)} %convolution_convert_fusion) | data formatting | bytes 18939904 | tf_op jit(solution)/shard_map/optimization_barrier | solution.py:231
  303.8 8.8 %convolution_convert_fusion.1 = bf16[1280,4352]{1,0:T(8,128)(2,1)} fusion(bf16[128,1280]{0,1:T(8,128)(2,1)} %bitcast.90, bf16[128,4352]{1,0:T(8,128)(2,1)} %get-tuple-element.11), kind=kOutput, calls=%fused_computation.2 | convolution fusion | flops 1431633920 | bytes 12582912 | tf_op jit(solution)/shard_map/na,nb->ab/dot_general | solution.py:49
  314.1 7.3 fusion.80
  328.8 3.7 convolution_convert_fusion.4
  341.8 15.5 %fusion.18 = f32[17,64,256]{2,1,0:T(8,128)} fusion(bf16[128,17,64]{0,2,1:T(8,128)(2,1)} %bitcast.105, f32[17,128,256]{2,1,0:T(8,128)} %fusion.81, f32[17,128,256]{2,1,0:T(8,128)S(1)} %get-tuple-element.45, f32[17,128]{1,0:T(8,128)S(1)} %copy-done.24, pred[128,256]{1,0:T(8,128)(4,1)S(1)} %fusion.44), kind=kOutput, calls=%fused_computation.34 | convolution fusion | flops 77433216 | bytes 5890560 | tf_op jit(solution)/shard_map/hqk,qhd->khd/dot_general | solution.py:268
  357.4 3.6 convolution_convert_fusion.3
  363.1 15.6 %fusion.76 = (bf16[17,64]{1,0:T(8,128)(2,1)S(1)}, bf16[128,17,64]{0,2,1:T(8,128)(2,1)}) fusion(bf16[256,17,64]{0,2,1:T(8,128)(2,1)} %bitcast.96, f32[17,128,256]{2,1,0:T(8,128)} %fusion.81, f32[17,128]{1,0:T(8,128)S(1)} %copy-done.24, f32[17,128,256]{2,1,0:T(8,128)S(1)} %get-tuple-element.45, pred[128,256]{1,0:T(8,128)(4,1)S(1)} %fusion.44), kind=kOutput, calls=%fused_computation.136 | convolution fusion | flops 77710656 | bytes 5335680 | tf_op jit(solution)/shard_map/hqk,khd->qhd/dot_general | solution.py:265
  381.9 2.5 convolution_convert_fusion.2
  384.4 4.8 pad_maximum_fusion
  389.2 14.8 %copy.39 = bf16[1280,4352]{1,0:T(8,128)(2,1)} copy(bf16[1280,4352]{0,1:T(8,128)(2,1)} %pad_maximum_fusion) | data formatting | bytes 22282240 | tf_op jit(solution)/shard_map/concatenate | solution.py:292
  404.2 5.8 fusion.1
  411.4 10.5 %pad_add_fusion = bf16[32,40,4352]{2,1,0:T(8,128)(2,1)} fusion(bf16[32,40,4352]{2,1,0:T(8,128)(2,1)} %bitcast.87, bf16[32,1,408]{2,1,0:T(2,128)(2,1)S(1)} %convert_element_type.173), kind=kLoop, calls=%fused_computation.5 | loop fusion | flops 22282240 | bytes 22308352 | tf_op jit(solution)/shard_map/add | solution.py:299
  423.6 8.2 %fusion.8 = bf16[1,128,1088]{1,2,0:T(8,128)(2,1)} fusion(f32[128,1088]{0,1:T(8,128)S(1)} %get-tuple-element.47, bf16[4352,1088]{1,0:T(8,128)(2,1)} %all-gather.8.cloned.1.call-done, f32[1088]{0:T(1024)S(1)} %add.198, f32[128,4352]{1,0:T(8,128)S(1)} %copy-done.2), kind=kOutput, calls=%fused_computation.21 | convolution fusion | flops 1217585152 | bytes 12538112 | tf_op jit(solution)/shard_map/dot_general | solution.py:216
  437.9 154.7 %reduce-scatter.8.cloned.1.call-done = bf16[1,40,4352]{2,1,0:T(8,128)(2,1)} async-done(((bf16[32,40,4352]{2,1,0:T(8,128)(2,1)}), bf16[1,40,4352]{2,1,0:T(8,128)(2,1)}) %reduce-scatter.8.cloned.1.call-update) | async-done | bytes 348176 | tf_op jit(solution)/shard_map/reduce_scatter | solution.py:101
  594.4 152.0 %reduce-scatter.6.cloned.1.call-done = bf16[1,40,4352]{2,1,0:T(8,128)(2,1)} async-done(((bf16[32,40,4352]{2,1,0:T(8,128)(2,1)}), bf16[1,40,4352]{2,1,0:T(8,128)(2,1)}) %reduce-scatter.6.cloned.1.call-update) | async-done | bytes 348176 | tf_op jit(solution)/shard_map/reduce_scatter | solution.py:101
  (176 shorter events, 64.0 us)
Async XLA Ops:
  7.2 4.0 copy-start.16
  7.2 5.2 copy-start.17
  7.2 97.4 %all-gather.4.cloned.1.call-start = ((), (), s32[]{:S(2)}) async-start(), calls=%async_computation.3 | async-start | bytes 11827200 | tf_op jit(solution)/shard_map/all_gather | solution.py:80
  11.2 184.6 %all-gather.6.cloned.1.call-start = ((), (), s32[]{:S(2)}) async-start(), calls=%async_computation.4 | async-start | bytes 11489280 | tf_op jit(solution)/shard_map/all_gather | solution.py:80
  12.3 269.0 %all-gather.8.cloned.1.call-start = ((), (), s32[]{:S(2)}) async-start(), calls=%async_computation.5 | async-start | bytes 10340352 | tf_op jit(solution)/shard_map/all_gather | solution.py:80
  13.4 422.3 %reduce-scatter.10.cloned.1.call-start = ((), (), s32[]{:S(2)}) async-start(), calls=%async_computation.8 | async-start | bytes 10340352
  13.9 93.7 %copy-start.28 = (f32[128]{0:T(128)}, f32[128]{0:T(128)S(1)}, u32[]{:S(2)}) copy-start(f32[128]{0:T(128)S(1)} %add_rsqrt_fusion.1) | copy-start | bytes 1540
  107.4 18.5 %copy-start.21 = (f32[8,136]{1,0:T(8,128)}, f32[8,136]{1,0:T(8,128)S(1)}, u32[]{:S(2)}) copy-start(f32[8,136]{1,0:T(8,128)S(1)} %get-tuple-element.21) | copy-start | bytes 13060
  108.5 7.0 copy-start.12
  115.9 5.3 copy-start.14
  118.1 4.0 copy-start.10
  195.7 7.4 copy-start.7
  303.8 288.8 %reduce-scatter.8.cloned.1.call-start = ((), (), s32[]{:S(2)}) async-start(), calls=%async_computation.7 | async-start | bytes 11489280 | tf_op jit(solution)/shard_map/reduce_scatter | solution.py:101
  312.7 433.7 %reduce-scatter.6.cloned.1.call-start = ((), (), s32[]{:S(2)}) async-start(), calls=%async_computation.6 | async-start | bytes 11489280 | tf_op jit(solution)/shard_map/reduce_scatter | solution.py:101
  321.4 3.6 copy-start.27
  321.4 3.6 copy-start.31
  322.9 3.5 copy-start.32
  328.8 7.4 copy-start.24
  336.2 3.7 copy-start.8
  336.2 3.7 copy-start.11
  339.7 39.5 %collective-permute-start.1 = (bf16[128,1088]{0,1:T(8,128)(2,1)}, bf16[128,1088]{0,1:T(8,128)(2,1)}, u32[]{:S(2)}, u32[]{:S(2)}) collective-permute-start(bf16[128,1088]{0,1:T(8,128)(2,1)} %dynamic-slice_convert_fusion), channel_id=1, source_target_pairs={{0,1},{1,0},{2,3},{3,2},{4,5},{5,4},{6,7},{7,6},{8,9},{9,8},{10,11... | collective-permute-start | bytes 835592 | tf_op jit(solution)/shard_map/ppermute | solution.py:124
  362.8 17.9 %collective-permute-start = (bf16[128,1088]{0,1:T(8,128)(2,1)}, bf16[128,1088]{0,1:T(8,128)(2,1)}, u32[]{:S(2)}, u32[]{:S(2)}) collective-permute-start(bf16[128,1088]{0,1:T(8,128)(2,1)} %dynamic-slice_convert_fusion.1), channel_id=1, source_target_pairs={{0,1},{1,0},{2,3},{3,2},{4,5},{5,4},{6,7},{7,6},{8,9},{9,8},{10,11... | collective-permute-start | bytes 835592 | tf_op jit(solution)/shard_map/ppermute | solution.py:124
  404.2 5.8 copy-start.29
  423.6 9.4 %copy-start.4 = (f32[128,1088]{0,1:T(8,128)S(1)}, f32[128,1088]{0,1:T(8,128)}, u32[]{:S(2)}) copy-start(f32[128,1088]{0,1:T(8,128)} %copy-done.3) | copy-start | bytes 1671172
  (19 other events, 34.3 us)
Sparse Core Ops, SparseCore 0:
  11.5 93.0 all-gather.3
  108.0 87.7 all-gather.5
  198.7 82.6 all-gather.7
  303.9 131.8 reduce-scatter.9
  437.9 154.6 reduce-scatter.7
  594.7 151.6 reduce-scatter.5
